TPU v7x, 256 devices: a whole 4x4x8 slice. The times are simulated.
256 devices in a mesh: dp: 32 (over y_hi, z, core), shard: 8 (over x, y_lo).
Axes of the slice: x: 4, y: 4 (y_hi: 2, y_lo: 2; y = y_hi * 2 + y_lo), z: 8, core: 2. Of those that a mesh axis runs over, the one named last changes fastest.
Arguments:
- resid_in: bfloat16 [4096, 8192], P('dp', 'shard'), may hold values from -6 to 6
- hidden: bfloat16 [4096, 28672], P('shard', 'dp'), may hold values from -6 to 6
- w_down: bfloat16 [28672, 8192], P('dp', 'shard'), may hold values from -0.03125 to 0.03125
- frozen: bfloat16 [4096, 8192], P(('dp', 'shard')), may hold values from -6 to 6
- steer: bfloat16 [8192], P('shard'), may hold values from -6 to 6
- forget_flags: int32 [16], replicated, may hold values from 0 to 1, as said below
Outputs:
- updated: bfloat16 [4096, 8192], P('dp', 'shard')
- grad_down: float32 [28672, 8192], P('dp', 'shard')
Inputs may be any that keep to these rules, and one draw needn't show every extreme that they name: `forget_flags`: exactly half of the 16 sequences are forget sequences.
All inputs are finite; a program needn't handle non-finite values.
Results may differ from a plain program's by a relative error of at most 0.0019.
Values may be sent and summed in bfloat16 or wider, within the bound.
A program may use at most 128 MiB of HBM per device.

v0:
```python
import math
import jax
import jax.numpy as jnp
from jax import lax
from jax.sharding import PartitionSpec as P

SEQ_LEN = 256
retain_weight = 2.0


def per_device(resid_in, hidden, w_down, frozen, steer, forget_flags):
    whole_hidden = lax.all_gather(hidden, "shard", axis=0, tiled=True)
    tok_rows = resid_in.shape[0]
    mlp_out = lax.psum_scatter(
        jnp.dot(whole_hidden, w_down, preferred_element_type=jnp.float32),
        "dp",
        scatter_dimension=0,
        tiled=True,
    )
    residual = resid_in.astype(jnp.float32) + mlp_out
    updated = residual.astype(jnp.bfloat16)
    target_rows = lax.all_to_all(frozen, "shard", split_axis=1, concat_axis=0, tiled=True)
    start_row = lax.axis_index("dp") * tok_rows
    seq_ids = (start_row + jnp.arange(tok_rows, dtype=jnp.int32)) // SEQ_LEN
    seq_match = seq_ids[:, None] == jnp.arange(forget_flags.shape[0], dtype=jnp.int32)[None, :]
    is_forget = jnp.sum(jnp.where(seq_match, forget_flags[None, :], 0), axis=1) > 0
    total_tokens = tok_rows * lax.axis_size("dp")
    target = jnp.where(
        is_forget[:, None], steer.astype(jnp.float32)[None, :], target_rows.astype(jnp.float32)
    )
    loss_weight = jnp.where(is_forget, 1.0, retain_weight).astype(jnp.float32)
    slopes = (loss_weight[:, None] * (residual - target) * (1.0 / math.sqrt(total_tokens))).astype(
        jnp.bfloat16
    )
    all_slopes = lax.all_gather(slopes, "dp", axis=0, tiled=True)
    grad_down = lax.dot_general(
        whole_hidden, all_slopes, (((0,), (0,)), ((), ())), preferred_element_type=jnp.float32
    )
    return (updated, grad_down)


def solution(mesh):
    in_specs = (
        P("dp", "shard"),
        P("shard", "dp"),
        P("dp", "shard"),
        P(("dp", "shard"), None),
        P("shard"),
        P(),
    )
    out_specs = (P("dp", "shard"), P("dp", "shard"))
    return jax.shard_map(
        per_device, mesh=mesh, in_specs=in_specs, out_specs=out_specs, check_vma=False
    )
```

profile of v0, /device:TPU:1, one launch (start us, length us, event | category | flops | bytes accessed | tf_op | source)
XLA Modules:
  0.0 531.7 jit_solution(17514021398669694060)
XLA Ops:
  7.2 0.0 copy-start
  7.2 0.0 all-gather.3.cloned.1.call-start
  7.2 0.7 all-gather.3.cloned.1.call-update
  7.9 0.0 reduce-scatter.2.cloned.1.call-start
  8.0 156.9 %all-gather.3.cloned.1.call-done = bf16[4096,896]{1,0:T(8,128)(2,1)} async-done(((bf16[512,896]{1,0:T(8,128)(2,1)}), bf16[4096,896]{1,0:T(8,128)(2,1)}) %all-gather.3.cloned.1.call-update) | async-done | bytes 7340048 | tf_op jit(solution)/shard_map/all_gather | solution.py:12
  164.9 0.0 copy-done
  164.9 14.3 %fusion.5 = f32[4096,1024]{1,0:T(8,128)} fusion(bf16[4096,896]{1,0:T(8,128)(2,1)} %all-gather.3.cloned.1.call-done, bf16[896,1024]{1,0:T(8,128)(2,1)S(1)} %copy-done), kind=kOutput, calls=%fused_computation.17 | convolution fusion | flops 7516192768 | bytes 25952256 | tf_op jit(solution)/shard_map/dot_general | solution.py:15
  179.2 0.0 copy-start.1
  179.2 0.0 copy-start.4
  179.2 0.0 copy-start.3
  179.2 0.0 copy-start.2
  179.2 0.0 reduce-scatter.2.cloned.1.call-update
  179.3 0.9 copy-done.1
  180.2 0.7 copy.14
  180.9 7.4 %all-to-all-start = ((bf16[16,8,1024]{2,0,1:T(8,128)(2,1)}), bf16[16,8,1024]{2,0,1:T(8,128)(2,1)S(1)}, u32[]{:S(2)}, u32[]{:S(2)}) async-start(bf16[16,8,1024]{2,0,1:T(8,128)(2,1)} %bitcast.21), calls=%async_computation.1 | async-start | bytes 524288 | tf_op jit(solution)/shard_map/all_to_all | solution.py:22
  188.2 0.0 all-gather.5.cloned.1.call-start
  188.3 0.0 copy-done.4
  188.3 0.1 select_reduce_fusion
  188.4 0.0 copy-done.3
  188.4 5.7 %all-to-all-done = bf16[16,8,1024]{2,0,1:T(8,128)(2,1)S(1)} async-done(((bf16[16,8,1024]{2,0,1:T(8,128)(2,1)}), bf16[16,8,1024]{2,0,1:T(8,128)(2,1)S(1)}, u32[]{:S(2)}, u32[]{:S(2)}) %all-to-all-start) | async-done | bytes 262176 | tf_op jit(solution)/shard_map/all_to_all | solution.py:22
  194.2 203.4 %reduce-scatter.2.cloned.1.call-done = f32[128,1024]{1,0:T(8,128)} async-done(((f32[4096,1024]{1,0:T(8,128)}), f32[128,1024]{1,0:T(8,128)}) %reduce-scatter.2.cloned.1.call-update) | async-done | bytes 524304 | tf_op jit(solution)/shard_map/reduce_scatter | solution.py:14
  397.6 0.0 copy-done.2
  397.6 2.0 fusion.3
  399.6 0.0 all-gather.5.cloned.1.call-update
  399.6 105.9 %all-gather.5.cloned.1.call-done = bf16[4096,1024]{1,0:T(8,128)(2,1)} async-done(((bf16[128,1024]{1,0:T(8,128)(2,1)}), bf16[4096,1024]{1,0:T(8,128)(2,1)}) %all-gather.5.cloned.1.call-update) | async-done | bytes 8388624 | tf_op jit(solution)/shard_map/all_gather | solution.py:35
  505.6 14.6 %convolution_bitcast_fusion = f32[896,1024]{0,1:T(8,128)} fusion(bf16[4096,1024]{1,0:T(8,128)(2,1)} %all-gather.5.cloned.1.call-done, bf16[4096,896]{1,0:T(8,128)(2,1)} %all-gather.3.cloned.1.call-done), kind=kOutput, calls=%fused_computation | convolution fusion | flops 7516192768 | bytes 19398656 | tf_op jit(solution)/shard_map/dot_general | solution.py:36
  520.2 5.0 copy.11
  (4 shorter events, 0.0 us)
Async XLA Ops:
  7.2 157.7 %copy-start = (bf16[896,1024]{1,0:T(8,128)(2,1)S(1)}, bf16[896,1024]{1,0:T(8,128)(2,1)}, u32[]{:S(2)}) copy-start(bf16[896,1024]{1,0:T(8,128)(2,1)} %param.8) | copy-start | bytes 5505028
  7.2 157.7 %all-gather.3.cloned.1.call-start = ((), (), s32[]{:S(2)}) async-start(), calls=%async_computation.2 | async-start | bytes 8257536 | tf_op jit(solution)/shard_map/all_gather | solution.py:12
  7.9 389.7 %reduce-scatter.2.cloned.1.call-start = ((), (), s32[]{:S(2)}) async-start(), calls=%async_computation.3 | async-start | bytes 17301504 | tf_op jit(solution)/shard_map/reduce_scatter | solution.py:14
  179.2 0.9 copy-start.1
  179.2 9.1 %copy-start.4 = (s32[16]{0:T(128)S(1)}, s32[16]{0:T(128)}, u32[]{:S(2)}) copy-start(s32[16]{0:T(128)} %param.11) | copy-start | bytes 196
  179.2 9.2 %copy-start.3 = (bf16[1024]{0:T(1024)(128)(2,1)S(1)}, bf16[1024]{0:T(1024)(128)(2,1)}, u32[]{:S(2)}) copy-start(bf16[1024]{0:T(1024)(128)(2,1)} %param.10) | copy-start | bytes 6148
  179.2 218.4 %copy-start.2 = (bf16[128,1024]{1,0:T(8,128)(2,1)S(1)}, bf16[128,1024]{1,0:T(8,128)(2,1)}, u32[]{:S(2)}) copy-start(bf16[128,1024]{1,0:T(8,128)(2,1)} %param.6) | copy-start | bytes 786436
  180.9 13.3 %all-to-all-start = ((bf16[16,8,1024]{2,0,1:T(8,128)(2,1)}), bf16[16,8,1024]{2,0,1:T(8,128)(2,1)S(1)}, u32[]{:S(2)}, u32[]{:S(2)}) async-start(bf16[16,8,1024]{2,0,1:T(8,128)(2,1)} %bitcast.21), calls=%async_computation.1 | async-start | bytes 524288 | tf_op jit(solution)/shard_map/all_to_all | solution.py:22
  188.2 317.3 %all-gather.5.cloned.1.call-start = ((), (), s32[]{:S(2)}) async-start(), calls=%async_computation.4 | async-start | bytes 8650752 | tf_op jit(solution)/shard_map/all_gather | solution.py:35
Sparse Core Ops, SparseCore 0:
  9.8 155.0 all-gather.2
  179.4 218.1 reduce-scatter.1
  401.3 104.1 all-gather.4
where the time goes:
time: 532 us
  waiting for transfers between devices  473 us (89%)
  matrix products  29 us (5%)
  between operations  13.8 us (3%)
  starting transfers between devices  7.47 us (1%)
  local copies, waits for them, and re-layouts  6.64 us (1%)
    reduce_scatter x1, waiting for transfers between devices, per_device(): lax.psum_scatter(jnp.dot(whole_hidden, w_down, preferred_element_type=jnp...  203 us
    all_gather x1, waiting for transfers between devices, per_device(): whole_hidden = lax.all_gather(hidden, 'shard', axis=0, tiled=True)  157 us
    all_gather x1, waiting for transfers between devices, per_device(): all_slopes = lax.all_gather(slopes, 'dp', axis=0, tiled=True)  106 us
    dot_general x1, matrix products, per_device(): lax.dot_general(whole_hidden, all_slopes, (((0,), (0,)), ((), ())), prefe...  14.6 us
    dot_general x1, matrix products, per_device(): jnp.dot(whole_hidden, w_down, preferred_element_type=jnp.float32)  14.3 us
  transfers between devices with their start and end apart: 4, of which 4 were waited for; matrix products, arithmetic and copies ran while one was open for 0% of the time, Pallas kernels for 0%

commit v1 on v0

--- a/solution.py
+++ b/solution.py
@@ -8,8 +8,15 @@
 retain_weight = 2.0
 
 
+def gather_over(x, axis, dim):
+    peers = lax.axis_size(axis)
+    pieces = jnp.stack([x for _ in range(peers)])
+    pieces = lax.all_to_all(pieces, axis, split_axis=0, concat_axis=0)
+    return jnp.concatenate(pieces, axis=dim)
+
+
 def per_device(resid_in, hidden, w_down, frozen, steer, forget_flags):
-    whole_hidden = lax.all_gather(hidden, "shard", axis=0, tiled=True)
+    whole_hidden = gather_over(hidden, "shard", 0)
     tok_rows = resid_in.shape[0]
     mlp_out = lax.psum_scatter(
         jnp.dot(whole_hidden, w_down, preferred_element_type=jnp.float32),

time: 532 us -> 466 us (0.88)
  waiting for transfers between devices: 473 us -> 320 us
  blocking collectives: 0 us -> 88.4 us
    all_gather x1 -> x0, waiting for transfers between devices: 157 us -> none  [per_device(): whole_hidden = lax.all_gather(hidden, 'shard', axis=0, tiled=True)]
    all_to_all x0 -> x1, blocking collectives: none -> 88.4 us  [gather_over(): pieces = lax.all_to_all(pieces, axis, split_axis=0, concat_axis=0)]
  transfers between devices with their start and end apart: 4 -> 3, of which waited for: 4 -> 3; matrix products, arithmetic and copies ran while one was open for 0% -> 0% of each run, Pallas kernels for 0% -> 0%
where the time goes in v1:
time: 466 us
  waiting for transfers between devices  320 us (69%)
  blocking collectives  88.4 us (19%)
  matrix products  26.3 us (6%)
  between operations  14.1 us (3%)
  local copies, waits for them, and re-layouts  11.8 us (3%)
    reduce_scatter x1, waiting for transfers between devices, per_device(): lax.psum_scatter(jnp.dot(whole_hidden, w_down, preferred_element_type=jnp...  208 us
    all_gather x1, waiting for transfers between devices, per_device(): all_slopes = lax.all_gather(slopes, 'dp', axis=0, tiled=True)  106 us
    all_to_all x1, blocking collectives, gather_over(): pieces = lax.all_to_all(pieces, axis, split_axis=0, concat_axis=0)  88.4 us
    dot_general x1, matrix products, per_device(): lax.dot_general(whole_hidden, all_slopes, (((0,), (0,)), ((), ())), prefe...  14.6 us
    dot_general x1, matrix products, per_device(): jnp.dot(whole_hidden, w_down, preferred_element_type=jnp.float32)  11.7 us
  transfers between devices with their start and end apart: 3, of which 3 were waited for; matrix products, arithmetic and copies ran while one was open for 0% of the time, Pallas kernels for 0%

profile of v1, /device:TPU:1, one launch (start us, length us, event | category | flops | bytes accessed | tf_op | source)
XLA Modules:
  0.0 465.8 jit_solution(6009387594556144117)
XLA Ops:
  7.2 0.0 copy-start
  7.2 0.0 reduce-scatter.2.cloned.1.call-start
  7.2 2.2 stack.2
  9.5 88.4 %all_to_all.18 = bf16[8,512,896]{2,1,0:T(8,128)(2,1)S(1)} all-to-all(bf16[8,512,896]{2,1,0:T(8,128)(2,1)S(1)} %stack.2), channel_id=1, replica_groups=mesh['dp'=32,'shard'=8] {'shard'}, dimensions={0} | all-to-all | bytes 14680064 | tf_op jit(solution)/shard_map/all_to_all | solution.py:14
  97.9 0.0 copy-start.1
  97.9 2.9 copy-done.1
  100.8 0.0 copy-done
  100.8 11.7 %fusion.5 = f32[4096,1024]{1,0:T(8,128)} fusion(bf16[4096,896]{1,0:T(8,128)(2,1)S(1)} %bitcast.23, bf16[896,1024]{1,0:T(8,128)(2,1)S(1)} %copy-done), kind=kOutput, calls=%fused_computation.17 | convolution fusion | flops 7516192768 | bytes 25952256 | tf_op jit(solution)/shard_map/dot_general | solution.py:22
  112.5 0.0 copy-start.2
  112.5 0.0 copy-start.5
  112.5 0.0 copy-start.4
  112.5 0.0 copy-start.3
  112.5 0.0 reduce-scatter.2.cloned.1.call-update
  112.5 0.9 copy-done.2
  113.4 0.7 copy.14
  114.2 3.4 all-to-all-start.1
  117.6 0.0 all-gather.2.cloned.1.call-start
  117.7 0.0 copy-done.5
  117.7 0.1 select_reduce_fusion
  117.8 0.0 copy-done.4
  117.8 5.6 %all-to-all-done.1 = bf16[16,8,1024]{2,0,1:T(8,128)(2,1)S(1)} async-done(((bf16[16,8,1024]{2,0,1:T(8,128)(2,1)}), bf16[16,8,1024]{2,0,1:T(8,128)(2,1)S(1)}, u32[]{:S(2)}, u32[]{:S(2)}) %all-to-all-start.1) | async-done | bytes 262176 | tf_op jit(solution)/shard_map/all_to_all | solution.py:29
  123.4 208.0 %reduce-scatter.2.cloned.1.call-done = f32[128,1024]{1,0:T(8,128)} async-done(((f32[4096,1024]{1,0:T(8,128)}), f32[128,1024]{1,0:T(8,128)}) %reduce-scatter.2.cloned.1.call-update) | async-done | bytes 524304 | tf_op jit(solution)/shard_map/reduce_scatter | solution.py:21
  331.4 0.0 copy-done.3
  331.4 2.0 fusion.3
  333.4 0.0 all-gather.2.cloned.1.call-update
  333.4 106.0 %all-gather.2.cloned.1.call-done = bf16[4096,1024]{1,0:T(8,128)(2,1)} async-done(((bf16[128,1024]{1,0:T(8,128)(2,1)}), bf16[4096,1024]{1,0:T(8,128)(2,1)}) %all-gather.2.cloned.1.call-update) | async-done | bytes 8388624 | tf_op jit(solution)/shard_map/all_gather | solution.py:42
  439.4 14.6 %convolution_bitcast_fusion = f32[896,1024]{0,1:T(8,128)} fusion(bf16[4096,1024]{1,0:T(8,128)(2,1)} %all-gather.2.cloned.1.call-done, bf16[4096,896]{1,0:T(8,128)(2,1)} %bitcast.24), kind=kOutput, calls=%fused_computation | convolution fusion | flops 7516192768 | bytes 19398656 | tf_op jit(solution)/shard_map/dot_general | solution.py:43
  454.0 5.0 %copy.11 = f32[896,1024]{1,0:T(8,128)} copy(f32[896,1024]{0,1:T(8,128)} %convolution_bitcast_fusion) | data formatting | bytes 7340032
  (4 shorter events, 0.0 us)
Async XLA Ops:
  7.2 93.6 %copy-start = (bf16[896,1024]{1,0:T(8,128)(2,1)S(1)}, bf16[896,1024]{1,0:T(8,128)(2,1)}, u32[]{:S(2)}) copy-start(bf16[896,1024]{1,0:T(8,128)(2,1)} %param.8) | copy-start | bytes 5505028
  7.2 324.2 %reduce-scatter.2.cloned.1.call-start = ((), (), s32[]{:S(2)}) async-start(), calls=%async_computation.3 | async-start | bytes 17301504 | tf_op jit(solution)/shard_map/reduce_scatter | solution.py:21
  97.9 2.9 copy-start.1
  112.5 0.9 copy-start.2
  112.5 5.2 %copy-start.5 = (s32[16]{0:T(128)S(1)}, s32[16]{0:T(128)}, u32[]{:S(2)}) copy-start(s32[16]{0:T(128)} %param.11) | copy-start | bytes 196
  112.5 5.3 %copy-start.4 = (bf16[1024]{0:T(1024)(128)(2,1)S(1)}, bf16[1024]{0:T(1024)(128)(2,1)}, u32[]{:S(2)}) copy-start(bf16[1024]{0:T(1024)(128)(2,1)} %param.10) | copy-start | bytes 6148
  112.5 218.9 %copy-start.3 = (bf16[128,1024]{1,0:T(8,128)(2,1)S(1)}, bf16[128,1024]{1,0:T(8,128)(2,1)}, u32[]{:S(2)}) copy-start(bf16[128,1024]{1,0:T(8,128)(2,1)} %param.6) | copy-start | bytes 786436
  114.2 9.2 %all-to-all-start.1 = ((bf16[16,8,1024]{2,0,1:T(8,128)(2,1)}), bf16[16,8,1024]{2,0,1:T(8,128)(2,1)S(1)}, u32[]{:S(2)}, u32[]{:S(2)}) async-start(bf16[16,8,1024]{2,0,1:T(8,128)(2,1)} %bitcast.22), calls=%async_computation.2 | async-start | bytes 524288 | tf_op jit(solution)/shard_map/all_to_all | solution.py:29
  117.6 321.8 %all-gather.2.cloned.1.call-start = ((), (), s32[]{:S(2)}) async-start(), calls=%async_computation.4 | async-start | bytes 8650752 | tf_op jit(solution)/shard_map/all_gather | solution.py:42
Sparse Core Ops, SparseCore 0:
  112.7 218.6 reduce-scatter.1
  335.1 104.2 all-gather.1

commit v2 on v0

--- a/solution.py
+++ b/solution.py
@@ -6,6 +6,12 @@
 
 SEQ_LEN = 256
 retain_weight = 2.0
+
+
+def trade_parts(array, mesh_axis, split, join):
+    pieces = jnp.split(array, lax.axis_size(mesh_axis), axis=split)
+    received = lax.all_to_all(jnp.stack(pieces), mesh_axis, 0, 0)
+    return jnp.concatenate(received, axis=join)
 
 
 def per_device(resid_in, hidden, w_down, frozen, steer, forget_flags):
@@ -19,7 +25,7 @@
     )
     residual = resid_in.astype(jnp.float32) + mlp_out
     updated = residual.astype(jnp.bfloat16)
-    target_rows = lax.all_to_all(frozen, "shard", split_axis=1, concat_axis=0, tiled=True)
+    target_rows = trade_parts(frozen, "shard", 1, 0)
     start_row = lax.axis_index("dp") * tok_rows
     seq_ids = (start_row + jnp.arange(tok_rows, dtype=jnp.int32)) // SEQ_LEN
     seq_match = seq_ids[:, None] == jnp.arange(forget_flags.shape[0], dtype=jnp.int32)[None, :]

time: 532 us -> 532 us (level)
  transfers between devices with their start and end apart: 4 -> 4, of which waited for: 4 -> 4; matrix products, arithmetic and copies ran while one was open for 0% -> 1% of each run, Pallas kernels for 0% -> 0%
where the time goes in v2:
time: 532 us
  waiting for transfers between devices  468 us (88%)
  matrix products  29 us (5%)
  between operations  13.8 us (3%)
  local copies, waits for them, and re-layouts  10.9 us (2%)
  starting transfers between devices  7.47 us (1%)
    reduce_scatter x1, waiting for transfers between devices, per_device(): lax.psum_scatter(jnp.dot(whole_hidden, w_down, preferred_element_type=jnp...  199 us
    all_gather x1, waiting for transfers between devices, per_device(): whole_hidden = lax.all_gather(hidden, 'shard', axis=0, tiled=True)  157 us
    all_gather x1, waiting for transfers between devices, per_device(): all_slopes = lax.all_gather(slopes, 'dp', axis=0, tiled=True)  106 us
    dot_general x1, matrix products, per_device(): lax.dot_general(whole_hidden, all_slopes, (((0,), (0,)), ((), ())), prefe...  14.6 us
    dot_general x1, matrix products, per_device(): jnp.dot(whole_hidden, w_down, preferred_element_type=jnp.float32)  14.3 us
  transfers between devices with their start and end apart: 4, of which 4 were waited for; matrix products, arithmetic and copies ran while one was open for 1% of the time, Pallas kernels for 0%

profile of v2, /device:TPU:1, one launch (start us, length us, event | category | flops | bytes accessed | tf_op | source)
XLA Modules:
  0.0 531.7 jit_solution(6417476668491619644)
XLA Ops:
  7.2 0.0 copy-start
  7.2 0.0 all-gather.3.cloned.1.call-start
  7.2 0.7 all-gather.3.cloned.1.call-update
  7.9 0.0 reduce-scatter.2.cloned.1.call-start
  8.0 156.9 %all-gather.3.cloned.1.call-done = bf16[4096,896]{1,0:T(8,128)(2,1)} async-done(((bf16[512,896]{1,0:T(8,128)(2,1)}), bf16[4096,896]{1,0:T(8,128)(2,1)}) %all-gather.3.cloned.1.call-update) | async-done | bytes 7340048 | tf_op jit(solution)/shard_map/all_gather | solution.py:18
  164.9 0.0 copy-done
  164.9 14.3 %fusion.5 = f32[4096,1024]{1,0:T(8,128)} fusion(bf16[4096,896]{1,0:T(8,128)(2,1)} %all-gather.3.cloned.1.call-done, bf16[896,1024]{1,0:T(8,128)(2,1)S(1)} %copy-done), kind=kOutput, calls=%fused_computation.24 | convolution fusion | flops 7516192768 | bytes 25952256 | tf_op jit(solution)/shard_map/dot_general | solution.py:21
  179.2 0.0 copy-start.1
  179.2 0.0 copy-start.4
  179.2 0.0 copy-start.3
  179.2 0.0 copy-start.2
  179.2 0.0 reduce-scatter.2.cloned.1.call-update
  179.3 0.9 copy-done.1
  180.2 0.6 bitcast_dynamic-update-slice_fusion.7
  180.8 0.6 bitcast_dynamic-update-slice_fusion.6
  181.4 0.6 bitcast_dynamic-update-slice_fusion.5
  182.0 0.6 bitcast_dynamic-update-slice_fusion.4
  182.6 0.6 bitcast_dynamic-update-slice_fusion.3
  183.2 0.6 bitcast_dynamic-update-slice_fusion.2
  183.9 0.6 bitcast_dynamic-update-slice_fusion.1
  184.5 0.6 bitcast_dynamic-update-slice_fusion
  185.1 7.4 %all-to-all-start = ((bf16[8,16,1024]{2,1,0:T(8,128)(2,1)}), bf16[8,16,1024]{2,1,0:T(8,128)(2,1)S(1)}, u32[]{:S(2)}, u32[]{:S(2)}) async-start(bf16[8,16,1024]{2,1,0:T(8,128)(2,1)} %bitcast_dynamic-update-slice_fusion), calls=%async_computation.1 | async-start | bytes 524288 | tf_op jit(solution)/shard_map/all_to_all | solution.py:13
  192.5 0.0 all-gather.5.cloned.1.call-start
  192.5 0.0 copy-done.4
  192.5 0.1 select_reduce_fusion
  192.6 0.0 copy-done.3
  192.7 5.7 %all-to-all-done = bf16[8,16,1024]{2,1,0:T(8,128)(2,1)S(1)} async-done(((bf16[8,16,1024]{2,1,0:T(8,128)(2,1)}), bf16[8,16,1024]{2,1,0:T(8,128)(2,1)S(1)}, u32[]{:S(2)}, u32[]{:S(2)}) %all-to-all-start) | async-done | bytes 262176 | tf_op jit(solution)/shard_map/all_to_all | solution.py:13
  198.4 199.2 %reduce-scatter.2.cloned.1.call-done = f32[128,1024]{1,0:T(8,128)} async-done(((f32[4096,1024]{1,0:T(8,128)}), f32[128,1024]{1,0:T(8,128)}) %reduce-scatter.2.cloned.1.call-update) | async-done | bytes 524304 | tf_op jit(solution)/shard_map/reduce_scatter | solution.py:20
  397.6 0.0 copy-done.2
  397.6 2.0 fusion.3
  399.6 0.0 all-gather.5.cloned.1.call-update
  399.6 105.9 %all-gather.5.cloned.1.call-done = bf16[4096,1024]{1,0:T(8,128)(2,1)} async-done(((bf16[128,1024]{1,0:T(8,128)(2,1)}), bf16[4096,1024]{1,0:T(8,128)(2,1)}) %all-gather.5.cloned.1.call-update) | async-done | bytes 8388624 | tf_op jit(solution)/shard_map/all_gather | solution.py:41
  505.6 14.6 %convolution_bitcast_fusion = f32[896,1024]{0,1:T(8,128)} fusion(bf16[4096,1024]{1,0:T(8,128)(2,1)} %all-gather.5.cloned.1.call-done, bf16[4096,896]{1,0:T(8,128)(2,1)} %all-gather.3.cloned.1.call-done), kind=kOutput, calls=%fused_computation | convolution fusion | flops 7516192768 | bytes 19398656 | tf_op jit(solution)/shard_map/dot_general | solution.py:42
  520.2 5.0 copy.9
  (4 shorter events, 0.0 us)
Async XLA Ops:
  7.2 157.7 %copy-start = (bf16[896,1024]{1,0:T(8,128)(2,1)S(1)}, bf16[896,1024]{1,0:T(8,128)(2,1)}, u32[]{:S(2)}) copy-start(bf16[896,1024]{1,0:T(8,128)(2,1)} %param.8) | copy-start | bytes 5505028
  7.2 157.7 %all-gather.3.cloned.1.call-start = ((), (), s32[]{:S(2)}) async-start(), calls=%async_computation.2 | async-start | bytes 8257536 | tf_op jit(solution)/shard_map/all_gather | solution.py:18
  7.9 389.7 %reduce-scatter.2.cloned.1.call-start = ((), (), s32[]{:S(2)}) async-start(), calls=%async_computation.3 | async-start | bytes 17301504 | tf_op jit(solution)/shard_map/reduce_scatter | solution.py:20
  179.2 0.9 copy-start.1
  179.2 13.3 %copy-start.4 = (s32[16]{0:T(128)S(1)}, s32[16]{0:T(128)}, u32[]{:S(2)}) copy-start(s32[16]{0:T(128)} %param.11) | copy-start | bytes 196
  179.2 13.4 %copy-start.3 = (bf16[1024]{0:T(1024)(128)(2,1)S(1)}, bf16[1024]{0:T(1024)(128)(2,1)}, u32[]{:S(2)}) copy-start(bf16[1024]{0:T(1024)(128)(2,1)} %param.10) | copy-start | bytes 6148
  179.2 218.4 %copy-start.2 = (bf16[128,1024]{1,0:T(8,128)(2,1)S(1)}, bf16[128,1024]{1,0:T(8,128)(2,1)}, u32[]{:S(2)}) copy-start(bf16[128,1024]{1,0:T(8,128)(2,1)} %param.6) | copy-start | bytes 786436
  185.1 13.3 %all-to-all-start = ((bf16[8,16,1024]{2,1,0:T(8,128)(2,1)}), bf16[8,16,1024]{2,1,0:T(8,128)(2,1)S(1)}, u32[]{:S(2)}, u32[]{:S(2)}) async-start(bf16[8,16,1024]{2,1,0:T(8,128)(2,1)} %bitcast_dynamic-update-slice_fusion), calls=%async_computation.1 | async-start | bytes 524288 | tf_op jit(solution)/shard_map/all_to_all | solution.py:13
  192.5 313.1 %all-gather.5.cloned.1.call-start = ((), (), s32[]{:S(2)}) async-start(), calls=%async_computation.4 | async-start | bytes 8650752 | tf_op jit(solution)/shard_map/all_gather | solution.py:41
Sparse Core Ops, SparseCore 0:
  9.8 155.0 all-gather.2
  179.4 218.1 reduce-scatter.1
  401.3 104.1 all-gather.4
